TPU v7x, 256 devices: a whole 4x4x8 slice. The times are simulated.
256 devices in a mesh: ctx: 64 (over z, x, core), heads: 4 (over y).
Axes of the slice: x: 4, y: 4, z: 8, core: 2. Of those that a mesh axis runs over, the one named last changes fastest.
Arguments:
- q_raw: bfloat16 [16384, 8192], P('ctx', 'heads'), may hold values from -60 to 60
- k_raw: bfloat16 [16384, 1024], P('ctx', 'heads'), may hold values from -60 to 60
- values: bfloat16 [16384, 1024], P('ctx', 'heads'), may hold values from -6 to 6
- saved_out: bfloat16 [16384, 8192], P('ctx', 'heads'), may hold values from -6 to 6
- out_grad: bfloat16 [16384, 8192], P('ctx', 'heads'), may hold values from -60 to 60
- q_gain: float32 [128], replicated, may hold values from 0.25 to 1.75
- k_gain: float32 [128], replicated, may hold values from 0.25 to 1.75
- ancestors: int32 [256, 32], P('ctx'), may hold values from -1 to 255, as said below
Outputs:
- dq_raw: bfloat16 [16384, 8192], P('ctx', 'heads')
- dk_raw: bfloat16 [16384, 1024], P('ctx', 'heads')
- dv: bfloat16 [16384, 1024], P('ctx', 'heads')
- q_gain_grad: float32 [128], replicated
- k_gain_grad: float32 [128], replicated
Inputs may be any that keep to these rules, and one draw needn't show every extreme that they name: `ancestors`: the forest is 8 trees of 32 blocks each; in tree order, tree k holds blocks (k * 32 + 256 / 64 + b) mod 256 for b = 0 to 31. Row b lists, in tree order, every block on the path from its tree's first block to b, ending with b itself, then -1s. The first 16 blocks of a tree form its prompt, each the child of the block before it; every other block's parent is a block earlier in its tree, from the prompt's last block on.
All inputs are finite; a program needn't handle non-finite values.
Results may differ from a plain program's by a relative error of at most 0.0069.
Values may be sent and summed in bfloat16 or wider, within the bound.
A program may use at most 64 MiB of HBM per device.

v0:
```python
import math
import jax
import jax.numpy as jnp
from jax import lax
from jax.sharding import PartitionSpec as P

TREE_DEV = 8
ROPE_BASE = 1000000.0
EPS = 1e-06


def passed_along(value, axis, steps):
    count = lax.axis_size(axis)
    pairs = [(source, (source + steps) % count) for source in range(count)]
    return lax.ppermute(value, axis, pairs)


def rope_tables(positions, head_dim):
    half_dim = head_dim // 2
    frequency = jnp.exp(
        jnp.arange(half_dim, dtype=jnp.float32) * (-2.0 * math.log(ROPE_BASE) / head_dim)
    )
    angles = positions.astype(jnp.float32)[:, None] * frequency[None, :]
    return (jnp.cos(angles), jnp.sin(angles))


def norm_rope(inputs, gain_vec, cos_table, sin_table):
    recip_rms = lax.rsqrt(jnp.mean(inputs * inputs, -1, keepdims=True) + EPS)
    scaled = inputs * recip_rms * gain_vec
    half_dim = inputs.shape[-1] // 2
    cos_part = cos_table[:, None, :]
    sin_part = sin_table[:, None, :]
    front_half = scaled[..., :half_dim]
    back_half = scaled[..., half_dim:]
    return jnp.concatenate(
        [
            front_half * cos_part - back_half * sin_part,
            back_half * cos_part + front_half * sin_part,
        ],
        -1,
    )


def norm_rope_back(inputs, gain_vec, cos_table, sin_table, upstream):
    half_dim = inputs.shape[-1] // 2
    cos_part = cos_table[:, None, :]
    sin_part = sin_table[:, None, :]
    front_half = upstream[..., :half_dim]
    back_half = upstream[..., half_dim:]
    unrotated = jnp.concatenate(
        [
            front_half * cos_part + back_half * sin_part,
            back_half * cos_part - front_half * sin_part,
        ],
        -1,
    )
    recip_rms = lax.rsqrt(jnp.mean(inputs * inputs, -1, keepdims=True) + EPS)
    normed = inputs * recip_rms
    gain_term = jnp.sum(unrotated * normed, axis=(0, 1))
    gain_grad = unrotated * gain_vec
    input_grad = recip_rms * (gain_grad - normed * jnp.mean(gain_grad * normed, -1, keepdims=True))
    return (input_grad, gain_term)


def on_device(q_raw, k_raw, values, saved_out, out_grad, q_gain, k_gain, ancestors):
    tokens_here = q_raw.shape[0]
    head_dim = q_gain.shape[0]
    kv_local = k_raw.shape[1] // head_dim
    group_size = q_raw.shape[1] // (kv_local * head_dim)
    block_count = ancestors.shape[0]
    block_len = tokens_here // block_count
    cycle_size = lax.axis_size("ctx")
    my_index = lax.axis_index("ctx")
    hop_count = TREE_DEV - 1
    inv_root = 1.0 / math.sqrt(head_dim)
    offsets = jnp.arange(block_len, dtype=jnp.int32)
    depth_count = jnp.sum((ancestors >= 0).astype(jnp.int32), 1)
    positions = (((depth_count - 1) * block_len)[:, None] + offsets[None, :]).reshape(tokens_here)
    cos_table, sin_table = rope_tables(positions, head_dim)
    q_float = q_raw.astype(jnp.float32).reshape(tokens_here, kv_local * group_size, head_dim)
    k_float = k_raw.astype(jnp.float32).reshape(tokens_here, kv_local, head_dim)
    q_rot = norm_rope(q_float, q_gain, cos_table, sin_table).astype(jnp.bfloat16)
    q_rot = q_rot.reshape(tokens_here, kv_local, group_size, head_dim)
    k_rot = norm_rope(k_float, k_gain, cos_table, sin_table).astype(jnp.bfloat16)
    v_heads = values.reshape(tokens_here, kv_local, head_dim)
    grad_heads = out_grad.reshape(tokens_here, kv_local, group_size, head_dim)
    out_heads = saved_out.reshape(tokens_here, kv_local, group_size, head_dim)
    row_delta = jnp.einsum(
        "ikgd,ikgd->kgi", grad_heads, out_heads, preferred_element_type=jnp.float32
    )
    key_value = jnp.stack((k_rot, v_heads), 1)
    local_tok = jnp.arange(tokens_here, dtype=jnp.int32)

    def visible(source):
        key_blocks = source * block_count + jnp.arange(block_count, dtype=jnp.int32)
        block_vis = jnp.any(ancestors[:, :, None] == key_blocks[None, None, :], axis=1)
        token_vis = jnp.repeat(jnp.repeat(block_vis, block_len, 0), block_len, 1)
        causal = (local_tok[None, :] <= local_tok[:, None]) | (source != my_index)
        return (token_vis & causal, jnp.any(block_vis))

    def scores_of(key_rot):
        return (
            jnp.einsum("ikgd,jkd->kgij", q_rot, key_rot, preferred_element_type=jnp.float32)
            * inv_root
        )

    def add_mass(exp_mass, key_rot, allowed):
        expo = jnp.where(allowed[None, None], jnp.exp(scores_of(key_rot)), 0.0)
        return exp_mass + jnp.sum(expo, -1)

    def accumulate(exp_mass, key_rot, allowed):
        return add_mass(exp_mass, key_rot, allowed)

    own_allowed, own_touched = visible(my_index)
    exp_mass = add_mass(
        jnp.zeros((kv_local, group_size, tokens_here), jnp.float32), k_rot, own_allowed
    )

    def forward_step(hop_index, loop_state):
        mass_now, moving = loop_state
        moving = passed_along(moving, "ctx", 1)
        allowed, touched = visible((my_index - hop_index) % cycle_size)
        return (accumulate(mass_now, moving, allowed), moving)

    exp_mass, _ = lax.fori_loop(1, hop_count + 1, forward_step, (exp_mass, k_rot))
    log_mass = jnp.log(exp_mass)

    def grad_terms(key_rot, val_rot, allowed):
        weights = jnp.where(
            allowed[None, None], jnp.exp(scores_of(key_rot) - log_mass[..., None]), 0.0
        )
        weights_low = weights.astype(jnp.bfloat16)
        grad_prob = jnp.einsum(
            "ikgd,jkd->kgij", grad_heads, val_rot, preferred_element_type=jnp.float32
        )
        dscore = (weights * (grad_prob - row_delta[..., None]) * inv_root).astype(jnp.bfloat16)
        dq_part = jnp.einsum("kgij,jkd->ikgd", dscore, key_rot, preferred_element_type=jnp.float32)
        dk_part = jnp.einsum("kgij,ikgd->jkd", dscore, q_rot, preferred_element_type=jnp.float32)
        dv_part = jnp.einsum(
            "kgij,ikgd->jkd", weights_low, grad_heads, preferred_element_type=jnp.float32
        )
        return (dq_part, jnp.stack((dk_part, dv_part), 1))

    def pair_terms(moving, allowed):
        return grad_terms(moving[:, 0], moving[:, 1], allowed)

    dq_acc, own_part = grad_terms(k_rot, v_heads, own_allowed)
    key_grads = own_part

    def back_step(hop_index, loop_state):
        dq_now, grads_now, moving = loop_state
        moving = passed_along(moving, "ctx", 1)
        source = (my_index - hop_index) % cycle_size
        allowed, touched = visible(source)
        dq_part, kv_part = pair_terms(moving, allowed)
        grads_now = passed_along(grads_now, "ctx", 1) + kv_part
        return (dq_now + dq_part, grads_now, moving)

    dq_acc, key_grads, _ = lax.fori_loop(
        1, hop_count + 1, back_step, (dq_acc, key_grads, key_value)
    )
    key_grads = passed_along(key_grads, "ctx", -hop_count)
    dq_rot = dq_acc.reshape(tokens_here, kv_local * group_size, head_dim)
    dq_input, q_gain_part = norm_rope_back(q_float, q_gain, cos_table, sin_table, dq_rot)
    dk_input, k_gain_part = norm_rope_back(k_float, k_gain, cos_table, sin_table, key_grads[:, 0])
    q_gain_grad, k_gain_grad = lax.psum((q_gain_part, k_gain_part), ("ctx", "heads"))
    dq_raw = dq_input.astype(jnp.bfloat16).reshape(tokens_here, kv_local * group_size * head_dim)
    dk_raw = dk_input.astype(jnp.bfloat16).reshape(tokens_here, kv_local * head_dim)
    dv = key_grads[:, 1].astype(jnp.bfloat16).reshape(tokens_here, kv_local * head_dim)
    return (dq_raw, dk_raw, dv, q_gain_grad, k_gain_grad)


def solution(mesh):
    in_specs = (
        P("ctx", "heads"),
        P("ctx", "heads"),
        P("ctx", "heads"),
        P("ctx", "heads"),
        P("ctx", "heads"),
        P(),
        P(),
        P("ctx", None),
    )
    out_specs = (P("ctx", "heads"), P("ctx", "heads"), P("ctx", "heads"), P(), P())
    return jax.shard_map(
        on_device, mesh=mesh, in_specs=in_specs, out_specs=out_specs, check_vma=False
    )
```

profile of v0, /device:TPU:1, one launch (start us, length us, event | category | flops | bytes accessed | tf_op | source)
XLA Modules:
  0.0 316.6 jit_solution(3900875006757037314)
XLA Ops:
  11.5 2.9 fusion.29
  14.4 59.1 %while.38 = (s32[]{:T(128)}, f32[2,8,256]{2,1,0:T(8,128)S(1)}, bf16[256,2,128]{2,0,1:T(8,128)(2,1)S(1)}, s32[4,32]{1,0:T(4,128)S(1)}, s32[]{:T(128)}, /*index=5*...) while((s32[]{:T(128)}, f32[2,8,256]{2,1,0:T(8,128)S(1)}, ...), condition=%wide.region_8.9_spmd.clone, body=%wide.region_5.8_spmd.clone.sunk | while | flops 271778816 | bytes 2167688 | solution.py:125
  14.4 2.6 collective-permute-start
  20.0 2.5 collective-permute-start
  23.1 4.9 %collective-permute-done = bf16[256,2,128]{2,0,1:T(8,128)(2,1)S(1)} collective-permute-done((bf16[256,2,128]{2,0,1:T(8,128)(2,1)S(1)}, bf16[256,2,128]{2,0,1:T(8,128)(2,1)S(1)}, u32[]{:S(2)}, u32[]{:S(2)}) %collective-permute-start) | collective-permute-done | bytes 131104 | tf_op jit(solution)/shard_map/while/body/eval_jaxpr/ppermute | solution.py:15
  29.8 7.1 %collective-permute-done = bf16[256,2,128]{2,0,1:T(8,128)(2,1)S(1)} collective-permute-done((bf16[256,2,128]{2,0,1:T(8,128)(2,1)S(1)}, bf16[256,2,128]{2,0,1:T(8,128)(2,1)S(1)}, u32[]{:S(2)}, u32[]{:S(2)}) %collective-permute-start) | collective-permute-done | bytes 131104 | tf_op jit(solution)/shard_map/while/body/eval_jaxpr/ppermute | solution.py:15
  38.7 7.1 %collective-permute-done = bf16[256,2,128]{2,0,1:T(8,128)(2,1)S(1)} collective-permute-done((bf16[256,2,128]{2,0,1:T(8,128)(2,1)S(1)}, bf16[256,2,128]{2,0,1:T(8,128)(2,1)S(1)}, u32[]{:S(2)}, u32[]{:S(2)}) %collective-permute-start) | collective-permute-done | bytes 131104 | tf_op jit(solution)/shard_map/while/body/eval_jaxpr/ppermute | solution.py:15
  47.5 7.1 %collective-permute-done = bf16[256,2,128]{2,0,1:T(8,128)(2,1)S(1)} collective-permute-done((bf16[256,2,128]{2,0,1:T(8,128)(2,1)S(1)}, bf16[256,2,128]{2,0,1:T(8,128)(2,1)S(1)}, u32[]{:S(2)}, u32[]{:S(2)}) %collective-permute-start) | collective-permute-done | bytes 131104 | tf_op jit(solution)/shard_map/while/body/eval_jaxpr/ppermute | solution.py:15
  56.4 7.1 %collective-permute-done = bf16[256,2,128]{2,0,1:T(8,128)(2,1)S(1)} collective-permute-done((bf16[256,2,128]{2,0,1:T(8,128)(2,1)S(1)}, bf16[256,2,128]{2,0,1:T(8,128)(2,1)S(1)}, u32[]{:S(2)}, u32[]{:S(2)}) %collective-permute-start) | collective-permute-done | bytes 131104 | tf_op jit(solution)/shard_map/while/body/eval_jaxpr/ppermute | solution.py:15
  65.3 7.1 %collective-permute-done = bf16[256,2,128]{2,0,1:T(8,128)(2,1)S(1)} collective-permute-done((bf16[256,2,128]{2,0,1:T(8,128)(2,1)S(1)}, bf16[256,2,128]{2,0,1:T(8,128)(2,1)S(1)}, u32[]{:S(2)}, u32[]{:S(2)}) %collective-permute-start) | collective-permute-done | bytes 131104 | tf_op jit(solution)/shard_map/while/body/eval_jaxpr/ppermute | solution.py:15
  79.2 3.3 %fusion.40 = f32[256,1,2,128]{0,3,2,1:T(8,128)S(1)} fusion(bf16[256,2,8,128]{0,3,2,1:T(8,128)(2,1)S(1)} %bitcast.262, f32[2,256,256,8]{2,1,3,0:T(8,128)} %get-tuple-element.597, f32[2,8,256]{2,1,0:T(8,128)S(1)} %copy-done.24, pred[256,256]{0,1:T(8,128)(4,1)S(1)} %copy-done.21), kind=kOutput, calls=%fused_computation.66 | convolution fusion | flops 272629760 | bytes 5586944 | tf_op jit(solution)/shard_map/kgij,ikgd->jkd/dot_general | solution.py:139
  89.9 1.9 copy.98
  95.2 123.4 %while.39 = (s32[]{:T(128)}, f32[256,2,8,128]{3,0,2,1:T(8,128)S(1)}, f32[256,2,2,128]{3,0,2,1:T(8,128)}, bf16[256,2,2,128]{3,0,2,1:T(8,128)(2,1)}, s32[4,32]{1,0...) while((s32[]{:T(128)}, ...), condition=%wide.region_11.12_spmd.clone, body=%wide.region_9.11_spmd.clone.sunk | while | flops 1354695680 | bytes 37999652 | solution.py:159
  96.9 6.4 %collective-permute-done.1 = bf16[256,2,2,128]{3,0,2,1:T(8,128)(2,1)S(1)} collective-permute-done((bf16[256,2,2,128]{3,0,2,1:T(8,128)(2,1)}, bf16[256,2,2,128]{3,0,2,1:T(8,128)(2,1)S(1)}, u32[]{:S(2)}, u32[]{:S(2)}) %collective-permute-start.1) | collective-permute-done | bytes 262176 | tf_op jit(solution)/shard_map/while/body/eval_jaxpr/ppermute | solution.py:15
  113.5 7.6 %collective-permute-done.1 = bf16[256,2,2,128]{3,0,2,1:T(8,128)(2,1)S(1)} collective-permute-done((bf16[256,2,2,128]{3,0,2,1:T(8,128)(2,1)}, bf16[256,2,2,128]{3,0,2,1:T(8,128)(2,1)S(1)}, u32[]{:S(2)}, u32[]{:S(2)}) %collective-permute-start.1) | collective-permute-done | bytes 262176 | tf_op jit(solution)/shard_map/while/body/eval_jaxpr/ppermute | solution.py:15
  131.3 7.6 %collective-permute-done.1 = bf16[256,2,2,128]{3,0,2,1:T(8,128)(2,1)S(1)} collective-permute-done((bf16[256,2,2,128]{3,0,2,1:T(8,128)(2,1)}, bf16[256,2,2,128]{3,0,2,1:T(8,128)(2,1)S(1)}, u32[]{:S(2)}, u32[]{:S(2)}) %collective-permute-start.1) | collective-permute-done | bytes 262176 | tf_op jit(solution)/shard_map/while/body/eval_jaxpr/ppermute | solution.py:15
  149.1 7.6 %collective-permute-done.1 = bf16[256,2,2,128]{3,0,2,1:T(8,128)(2,1)S(1)} collective-permute-done((bf16[256,2,2,128]{3,0,2,1:T(8,128)(2,1)}, bf16[256,2,2,128]{3,0,2,1:T(8,128)(2,1)S(1)}, u32[]{:S(2)}, u32[]{:S(2)}) %collective-permute-start.1) | collective-permute-done | bytes 262176 | tf_op jit(solution)/shard_map/while/body/eval_jaxpr/ppermute | solution.py:15
  166.9 7.6 %collective-permute-done.1 = bf16[256,2,2,128]{3,0,2,1:T(8,128)(2,1)S(1)} collective-permute-done((bf16[256,2,2,128]{3,0,2,1:T(8,128)(2,1)}, bf16[256,2,2,128]{3,0,2,1:T(8,128)(2,1)S(1)}, u32[]{:S(2)}, u32[]{:S(2)}) %collective-permute-start.1) | collective-permute-done | bytes 262176 | tf_op jit(solution)/shard_map/while/body/eval_jaxpr/ppermute | solution.py:15
  184.7 7.6 %collective-permute-done.1 = bf16[256,2,2,128]{3,0,2,1:T(8,128)(2,1)S(1)} collective-permute-done((bf16[256,2,2,128]{3,0,2,1:T(8,128)(2,1)}, bf16[256,2,2,128]{3,0,2,1:T(8,128)(2,1)S(1)}, u32[]{:S(2)}, u32[]{:S(2)}) %collective-permute-start.1) | collective-permute-done | bytes 262176 | tf_op jit(solution)/shard_map/while/body/eval_jaxpr/ppermute | solution.py:15
  202.5 7.6 %collective-permute-done.1 = bf16[256,2,2,128]{3,0,2,1:T(8,128)(2,1)S(1)} collective-permute-done((bf16[256,2,2,128]{3,0,2,1:T(8,128)(2,1)}, bf16[256,2,2,128]{3,0,2,1:T(8,128)(2,1)S(1)}, u32[]{:S(2)}, u32[]{:S(2)}) %collective-permute-start.1) | collective-permute-done | bytes 262176 | tf_op jit(solution)/shard_map/while/body/eval_jaxpr/ppermute | solution.py:15
  220.2 2.5 multiply_add_fusion
  222.7 2.1 multiply_reduce_fusion.1
  226.0 3.8 %fusion.36 = (f32[2048]{0:T(1024)S(1)}, bf16[256,2048]{1,0:T(8,128)(2,1)}) fusion(bf16[256,2048]{1,0:T(8,128)(2,1)S(1)} %copy-done.3, f32[32,8,16,128]{3,2,1,0:T(8,128)S(1)} %bitcast.265, f32[32,8,16,128]{3,2,1,0:T(8,128)S(1)} %bitcast.267, f32[32,8,16,128]{3,2,1,0:T(8,128)S(1)} %bitcast.266, f32[2048]{0:T(1024)S(1)} %broadcast_bitcast_fusion), kind=kLoop, calls=%fused_computation.53 | loop fusion | flops 4716544 | bytes 8404992 | tf_op jit(solution)/shard_map/reduce_sum | solution.py:59
  232.6 84.0 %all-reduce = (f32[128]{0:T(128)}, f32[128]{0:T(128)}) all-reduce(f32[128]{0:T(128)S(1)} %bitcast_reduce_fusion, f32[128]{0:T(128)S(1)} %bitcast_reduce_fusion.1), channel_id=1, replica_groups=mesh['ctx'=64,'heads'=4] {'ctx','heads'}, use_global_device_ids=true, to_apply=%region_16.17 | all-reduce | flops 256 | bytes 2048 | tf_op jit(solution)/shard_map/psum | solution.py:166
  (344 shorter events, 116.3 us)
Async XLA Ops:
  1.8 5.1 %copy-start.6 = (f32[256,2,128]{2,0,1:T(8,128)}, f32[256,2,128]{2,0,1:T(8,128)S(1)}, u32[]{:S(2)}) copy-start(f32[256,2,128]{2,0,1:T(8,128)S(1)} %copy.83) | copy-start | bytes 786436
  14.4 59.7 %copy-start.14 = (bf16[256,2048]{1,0:T(8,128)(2,1)S(1)}, bf16[256,2048]{1,0:T(8,128)(2,1)}, u32[]{:S(2)}) copy-start(bf16[256,2048]{1,0:T(8,128)(2,1)} %param.16) | copy-start | bytes 3145732
  14.4 4.5 %collective-permute-start = (bf16[256,2,128]{2,0,1:T(8,128)(2,1)S(1)}, bf16[256,2,128]{2,0,1:T(8,128)(2,1)S(1)}, u32[]{:S(2)}, u32[]{:S(2)}) collective-permute-start(bf16[256,2,128]{2,0,1:T(8,128)(2,1)S(1)} %get-tuple-element.709), channel_id=1, source_target_pairs={{0,4},{4,8},{8,12},{12,16},{16,20},{20,24},{24,28},{28,32},{32,36}... | collective-permute-start | bytes 393224 | tf_op jit(solution)/shard_map/while/body/eval_jaxpr/ppermute | solution.py:15
  20.0 8.0 %collective-permute-start = (bf16[256,2,128]{2,0,1:T(8,128)(2,1)S(1)}, bf16[256,2,128]{2,0,1:T(8,128)(2,1)S(1)}, u32[]{:S(2)}, u32[]{:S(2)}) collective-permute-start(bf16[256,2,128]{2,0,1:T(8,128)(2,1)S(1)} %get-tuple-element.709), channel_id=1, source_target_pairs={{0,4},{4,8},{8,12},{12,16},{16,20},{20,24},{24,28},{28,32},{32,36}... | collective-permute-start | bytes 393224 | tf_op jit(solution)/shard_map/while/body/eval_jaxpr/ppermute | solution.py:15
  29.1 7.8 %collective-permute-start = (bf16[256,2,128]{2,0,1:T(8,128)(2,1)S(1)}, bf16[256,2,128]{2,0,1:T(8,128)(2,1)S(1)}, u32[]{:S(2)}, u32[]{:S(2)}) collective-permute-start(bf16[256,2,128]{2,0,1:T(8,128)(2,1)S(1)} %get-tuple-element.709), channel_id=1, source_target_pairs={{0,4},{4,8},{8,12},{12,16},{16,20},{20,24},{24,28},{28,32},{32,36}... | collective-permute-start | bytes 393224 | tf_op jit(solution)/shard_map/while/body/eval_jaxpr/ppermute | solution.py:15
  38.0 7.8 %collective-permute-start = (bf16[256,2,128]{2,0,1:T(8,128)(2,1)S(1)}, bf16[256,2,128]{2,0,1:T(8,128)(2,1)S(1)}, u32[]{:S(2)}, u32[]{:S(2)}) collective-permute-start(bf16[256,2,128]{2,0,1:T(8,128)(2,1)S(1)} %get-tuple-element.709), channel_id=1, source_target_pairs={{0,4},{4,8},{8,12},{12,16},{16,20},{20,24},{24,28},{28,32},{32,36}... | collective-permute-start | bytes 393224 | tf_op jit(solution)/shard_map/while/body/eval_jaxpr/ppermute | solution.py:15
  46.9 7.8 %collective-permute-start = (bf16[256,2,128]{2,0,1:T(8,128)(2,1)S(1)}, bf16[256,2,128]{2,0,1:T(8,128)(2,1)S(1)}, u32[]{:S(2)}, u32[]{:S(2)}) collective-permute-start(bf16[256,2,128]{2,0,1:T(8,128)(2,1)S(1)} %get-tuple-element.709), channel_id=1, source_target_pairs={{0,4},{4,8},{8,12},{12,16},{16,20},{20,24},{24,28},{28,32},{32,36}... | collective-permute-start | bytes 393224 | tf_op jit(solution)/shard_map/while/body/eval_jaxpr/ppermute | solution.py:15
  55.7 7.8 %collective-permute-start = (bf16[256,2,128]{2,0,1:T(8,128)(2,1)S(1)}, bf16[256,2,128]{2,0,1:T(8,128)(2,1)S(1)}, u32[]{:S(2)}, u32[]{:S(2)}) collective-permute-start(bf16[256,2,128]{2,0,1:T(8,128)(2,1)S(1)} %get-tuple-element.709), channel_id=1, source_target_pairs={{0,4},{4,8},{8,12},{12,16},{16,20},{20,24},{24,28},{28,32},{32,36}... | collective-permute-start | bytes 393224 | tf_op jit(solution)/shard_map/while/body/eval_jaxpr/ppermute | solution.py:15
  64.6 7.8 %collective-permute-start = (bf16[256,2,128]{2,0,1:T(8,128)(2,1)S(1)}, bf16[256,2,128]{2,0,1:T(8,128)(2,1)S(1)}, u32[]{:S(2)}, u32[]{:S(2)}) collective-permute-start(bf16[256,2,128]{2,0,1:T(8,128)(2,1)S(1)} %get-tuple-element.709), channel_id=1, source_target_pairs={{0,4},{4,8},{8,12},{12,16},{16,20},{20,24},{24,28},{28,32},{32,36}... | collective-permute-start | bytes 393224 | tf_op jit(solution)/shard_map/while/body/eval_jaxpr/ppermute | solution.py:15
  95.2 8.1 %collective-permute-start.1 = (bf16[256,2,2,128]{3,0,2,1:T(8,128)(2,1)}, bf16[256,2,2,128]{3,0,2,1:T(8,128)(2,1)S(1)}, u32[]{:S(2)}, u32[]{:S(2)}) collective-permute-start(bf16[256,2,2,128]{3,0,2,1:T(8,128)(2,1)} %get-tuple-element.747), channel_id=1, source_target_pairs={{0,4},{4,8},{8,12},{12,16},{16,20},{20,24},{24,28},{28,32},{32,36}... | collective-permute-start | bytes 786440 | tf_op jit(solution)/shard_map/while/body/eval_jaxpr/ppermute | solution.py:15
  95.2 14.7 %collective-permute-start.2 = (f32[256,2,2,128]{3,0,2,1:T(8,128)}, f32[256,2,2,128]{3,0,2,1:T(8,128)}, u32[]{:S(2)}, u32[]{:S(2)}) collective-permute-start(f32[256,2,2,128]{3,0,2,1:T(8,128)} %get-tuple-element.746), channel_id=1, source_target_pairs={{0,4},{4,8},{8,12},{12,16},{16,20},{20,24},{24,28},{28,32},{32,36}... | collective-permute-start | bytes 1572872 | tf_op jit(solution)/shard_map/while/body/eval_jaxpr/ppermute | solution.py:15
  111.8 9.3 %collective-permute-start.1 = (bf16[256,2,2,128]{3,0,2,1:T(8,128)(2,1)}, bf16[256,2,2,128]{3,0,2,1:T(8,128)(2,1)S(1)}, u32[]{:S(2)}, u32[]{:S(2)}) collective-permute-start(bf16[256,2,2,128]{3,0,2,1:T(8,128)(2,1)} %get-tuple-element.747), channel_id=1, source_target_pairs={{0,4},{4,8},{8,12},{12,16},{16,20},{20,24},{24,28},{28,32},{32,36}... | collective-permute-start | bytes 786440 | tf_op jit(solution)/shard_map/while/body/eval_jaxpr/ppermute | solution.py:15
  111.8 15.9 %collective-permute-start.2 = (f32[256,2,2,128]{3,0,2,1:T(8,128)}, f32[256,2,2,128]{3,0,2,1:T(8,128)}, u32[]{:S(2)}, u32[]{:S(2)}) collective-permute-start(f32[256,2,2,128]{3,0,2,1:T(8,128)} %get-tuple-element.746), channel_id=1, source_target_pairs={{0,4},{4,8},{8,12},{12,16},{16,20},{20,24},{24,28},{28,32},{32,36}... | collective-permute-start | bytes 1572872 | tf_op jit(solution)/shard_map/while/body/eval_jaxpr/ppermute | solution.py:15
  129.6 9.3 %collective-permute-start.1 = (bf16[256,2,2,128]{3,0,2,1:T(8,128)(2,1)}, bf16[256,2,2,128]{3,0,2,1:T(8,128)(2,1)S(1)}, u32[]{:S(2)}, u32[]{:S(2)}) collective-permute-start(bf16[256,2,2,128]{3,0,2,1:T(8,128)(2,1)} %get-tuple-element.747), channel_id=1, source_target_pairs={{0,4},{4,8},{8,12},{12,16},{16,20},{20,24},{24,28},{28,32},{32,36}... | collective-permute-start | bytes 786440 | tf_op jit(solution)/shard_map/while/body/eval_jaxpr/ppermute | solution.py:15
  129.6 15.9 %collective-permute-start.2 = (f32[256,2,2,128]{3,0,2,1:T(8,128)}, f32[256,2,2,128]{3,0,2,1:T(8,128)}, u32[]{:S(2)}, u32[]{:S(2)}) collective-permute-start(f32[256,2,2,128]{3,0,2,1:T(8,128)} %get-tuple-element.746), channel_id=1, source_target_pairs={{0,4},{4,8},{8,12},{12,16},{16,20},{20,24},{24,28},{28,32},{32,36}... | collective-permute-start | bytes 1572872 | tf_op jit(solution)/shard_map/while/body/eval_jaxpr/ppermute | solution.py:15
  147.4 9.3 %collective-permute-start.1 = (bf16[256,2,2,128]{3,0,2,1:T(8,128)(2,1)}, bf16[256,2,2,128]{3,0,2,1:T(8,128)(2,1)S(1)}, u32[]{:S(2)}, u32[]{:S(2)}) collective-permute-start(bf16[256,2,2,128]{3,0,2,1:T(8,128)(2,1)} %get-tuple-element.747), channel_id=1, source_target_pairs={{0,4},{4,8},{8,12},{12,16},{16,20},{20,24},{24,28},{28,32},{32,36}... | collective-permute-start | bytes 786440 | tf_op jit(solution)/shard_map/while/body/eval_jaxpr/ppermute | solution.py:15
  147.4 15.9 %collective-permute-start.2 = (f32[256,2,2,128]{3,0,2,1:T(8,128)}, f32[256,2,2,128]{3,0,2,1:T(8,128)}, u32[]{:S(2)}, u32[]{:S(2)}) collective-permute-start(f32[256,2,2,128]{3,0,2,1:T(8,128)} %get-tuple-element.746), channel_id=1, source_target_pairs={{0,4},{4,8},{8,12},{12,16},{16,20},{20,24},{24,28},{28,32},{32,36}... | collective-permute-start | bytes 1572872 | tf_op jit(solution)/shard_map/while/body/eval_jaxpr/ppermute | solution.py:15
  165.2 9.3 %collective-permute-start.1 = (bf16[256,2,2,128]{3,0,2,1:T(8,128)(2,1)}, bf16[256,2,2,128]{3,0,2,1:T(8,128)(2,1)S(1)}, u32[]{:S(2)}, u32[]{:S(2)}) collective-permute-start(bf16[256,2,2,128]{3,0,2,1:T(8,128)(2,1)} %get-tuple-element.747), channel_id=1, source_target_pairs={{0,4},{4,8},{8,12},{12,16},{16,20},{20,24},{24,28},{28,32},{32,36}... | collective-permute-start | bytes 786440 | tf_op jit(solution)/shard_map/while/body/eval_jaxpr/ppermute | solution.py:15
  165.2 15.9 %collective-permute-start.2 = (f32[256,2,2,128]{3,0,2,1:T(8,128)}, f32[256,2,2,128]{3,0,2,1:T(8,128)}, u32[]{:S(2)}, u32[]{:S(2)}) collective-permute-start(f32[256,2,2,128]{3,0,2,1:T(8,128)} %get-tuple-element.746), channel_id=1, source_target_pairs={{0,4},{4,8},{8,12},{12,16},{16,20},{20,24},{24,28},{28,32},{32,36}... | collective-permute-start | bytes 1572872 | tf_op jit(solution)/shard_map/while/body/eval_jaxpr/ppermute | solution.py:15
  183.0 9.3 %collective-permute-start.1 = (bf16[256,2,2,128]{3,0,2,1:T(8,128)(2,1)}, bf16[256,2,2,128]{3,0,2,1:T(8,128)(2,1)S(1)}, u32[]{:S(2)}, u32[]{:S(2)}) collective-permute-start(bf16[256,2,2,128]{3,0,2,1:T(8,128)(2,1)} %get-tuple-element.747), channel_id=1, source_target_pairs={{0,4},{4,8},{8,12},{12,16},{16,20},{20,24},{24,28},{28,32},{32,36}... | collective-permute-start | bytes 786440 | tf_op jit(solution)/shard_map/while/body/eval_jaxpr/ppermute | solution.py:15
  183.0 15.9 %collective-permute-start.2 = (f32[256,2,2,128]{3,0,2,1:T(8,128)}, f32[256,2,2,128]{3,0,2,1:T(8,128)}, u32[]{:S(2)}, u32[]{:S(2)}) collective-permute-start(f32[256,2,2,128]{3,0,2,1:T(8,128)} %get-tuple-element.746), channel_id=1, source_target_pairs={{0,4},{4,8},{8,12},{12,16},{16,20},{20,24},{24,28},{28,32},{32,36}... | collective-permute-start | bytes 1572872 | tf_op jit(solution)/shard_map/while/body/eval_jaxpr/ppermute | solution.py:15
  200.8 9.3 %collective-permute-start.1 = (bf16[256,2,2,128]{3,0,2,1:T(8,128)(2,1)}, bf16[256,2,2,128]{3,0,2,1:T(8,128)(2,1)S(1)}, u32[]{:S(2)}, u32[]{:S(2)}) collective-permute-start(bf16[256,2,2,128]{3,0,2,1:T(8,128)(2,1)} %get-tuple-element.747), channel_id=1, source_target_pairs={{0,4},{4,8},{8,12},{12,16},{16,20},{20,24},{24,28},{28,32},{32,36}... | collective-permute-start | bytes 786440 | tf_op jit(solution)/shard_map/while/body/eval_jaxpr/ppermute | solution.py:15
  200.8 15.9 %collective-permute-start.2 = (f32[256,2,2,128]{3,0,2,1:T(8,128)}, f32[256,2,2,128]{3,0,2,1:T(8,128)}, u32[]{:S(2)}, u32[]{:S(2)}) collective-permute-start(f32[256,2,2,128]{3,0,2,1:T(8,128)} %get-tuple-element.746), channel_id=1, source_target_pairs={{0,4},{4,8},{8,12},{12,16},{16,20},{20,24},{24,28},{28,32},{32,36}... | collective-permute-start | bytes 1572872 | tf_op jit(solution)/shard_map/while/body/eval_jaxpr/ppermute | solution.py:15
  218.6 11.3 %collective-permute-start.3 = (f32[256,2,2,128]{3,0,2,1:T(8,128)}, f32[256,2,2,128]{3,0,2,1:T(8,128)S(1)}, u32[]{:S(2)}, u32[]{:S(2)}) collective-permute-start(f32[256,2,2,128]{3,0,2,1:T(8,128)} %get-tuple-element.450), channel_id=1, source_target_pairs={{0,228},{4,232},{8,236},{12,240},{16,244},{20,248},{24,252},{28,0}... | collective-permute-start | bytes 1572872 | tf_op jit(solution)/shard_map/ppermute | solution.py:15
  (47 other events, 81.6 us)
where the time goes:
time: 318 us; the launch traced here: 317 us
  waiting for transfers between devices  94.1 us (30%)
  blocking collectives  84 us (26%)
  matrix products  54.6 us (17%)
  other arithmetic  39.4 us (12%)
  local copies, waits for them, and re-layouts  36.9 us (12%)
  starting transfers between devices  5.57 us (2%)
    ppermute x22, waiting for transfers between devices, passed_along(): return lax.ppermute(value, axis, pairs)  94.1 us
    psum x1, blocking collectives, on_device(): lax.psum((q_gain_part, k_gain_part), ('ctx', 'heads'))  84 us
    dot_general x15, matrix products, scores_of(): jnp.einsum('ikgd,jkd->kgij', q_rot, key_rot, preferred_element_type=jnp.f...  15 us
    unnamed x68, local copies, waits for them, and re-layouts  13.6 us
    add x7, other arithmetic, back_step(): grads_now = passed_along(grads_now, 'ctx', 1) + kv_part  13.4 us
    dot_general x8, matrix products, grad_terms(): jnp.einsum('ikgd,jkd->kgij', grad_heads, val_rot, preferred_element_type=...  12.1 us
    dot_general x8, matrix products, grad_terms(): jnp.einsum('kgij,jkd->ikgd', dscore, key_rot, preferred_element_type=jnp....  11.6 us
    dot_general x8, matrix products, grad_terms(): jnp.einsum('kgij,ikgd->jkd', weights_low, grad_heads, preferred_element_t...  10 us
  transfers between devices with their start and end apart: 22, of which 14 were waited for; matrix products, arithmetic and copies ran while one was open for 22% of the time, Pallas kernels for 0%

commit v1 on v0

--- a/solution.py
+++ b/solution.py
@@ -163,7 +163,7 @@
     dq_rot = dq_acc.reshape(tokens_here, kv_local * group_size, head_dim)
     dq_input, q_gain_part = norm_rope_back(q_float, q_gain, cos_table, sin_table, dq_rot)
     dk_input, k_gain_part = norm_rope_back(k_float, k_gain, cos_table, sin_table, key_grads[:, 0])
-    q_gain_grad, k_gain_grad = lax.psum((q_gain_part, k_gain_part), ("ctx", "heads"))
+    q_gain_grad, k_gain_grad = lax.psum(lax.psum((q_gain_part, k_gain_part), "heads"), "ctx")
     dq_raw = dq_input.astype(jnp.bfloat16).reshape(tokens_here, kv_local * group_size * head_dim)
     dk_raw = dk_input.astype(jnp.bfloat16).reshape(tokens_here, kv_local * head_dim)
     dv = key_grads[:, 1].astype(jnp.bfloat16).reshape(tokens_here, kv_local * head_dim)

time: 318 us -> 380 us (1.19)
  blocking collectives: 84 us -> 143 us
    psum x1 -> x2, blocking collectives: 84 us -> 143 us  [the longest x1 134 us: on_device(): lax.psum(lax.psum((q_gain_part, k_gain_part), 'heads'), 'ctx')]
    unnamed x68 -> x72, local copies, waits for them, and re-layouts: 13.6 us -> 14.1 us
  transfers between devices with their start and end apart: 22 -> 22, of which waited for: 14 -> 14; matrix products, arithmetic and copies ran while one was open for 22% -> 18% of each run, Pallas kernels for 0% -> 0%
where the time goes in v1:
time: 380 us; the launch traced here: 379 us
  blocking collectives  143 us (38%)
  waiting for transfers between devices  94 us (25%)
  matrix products  54.6 us (14%)
  other arithmetic  40.2 us (11%)
  local copies, waits for them, and re-layouts  39.3 us (10%)
  starting transfers between devices  5.64 us (1%)
    psum x1, blocking collectives, on_device(): lax.psum(lax.psum((q_gain_part, k_gain_part), 'heads'), 'ctx')  134 us
    ppermute x22, waiting for transfers between devices, passed_along(): return lax.ppermute(value, axis, pairs)  94 us
    dot_general x15, matrix products, scores_of(): jnp.einsum('ikgd,jkd->kgij', q_rot, key_rot, preferred_element_type=jnp.f...  15 us
    unnamed x72, local copies, waits for them, and re-layouts  14.1 us
    add x7, other arithmetic, back_step(): grads_now = passed_along(grads_now, 'ctx', 1) + kv_part  13.4 us
    dot_general x8, matrix products, grad_terms(): jnp.einsum('ikgd,jkd->kgij', grad_heads, val_rot, preferred_element_type=...  12.1 us
    dot_general x8, matrix products, grad_terms(): jnp.einsum('kgij,jkd->ikgd', dscore, key_rot, preferred_element_type=jnp....  11.6 us
    dot_general x8, matrix products, grad_terms(): jnp.einsum('kgij,ikgd->jkd', weights_low, grad_heads, preferred_element_t...  10 us
  transfers between devices with their start and end apart: 22, of which 14 were waited for; matrix products, arithmetic and copies ran while one was open for 18% of the time, Pallas kernels for 0%

profile of v1, /device:TPU:1, one launch (start us, length us, event | category | flops | bytes accessed | tf_op | source)
XLA Modules:
  0.0 378.6 jit_solution(308510127077983583)
XLA Ops:
  11.5 2.9 fusion.29
  14.4 59.1 %while.38 = (s32[]{:T(128)}, f32[2,8,256]{2,1,0:T(8,128)S(1)}, bf16[256,2,128]{2,0,1:T(8,128)(2,1)S(1)}, s32[4,32]{1,0:T(4,128)S(1)}, s32[]{:T(128)}, /*index=5*...) while((s32[]{:T(128)}, f32[2,8,256]{2,1,0:T(8,128)S(1)}, ...), condition=%wide.region_8.9_spmd.clone, body=%wide.region_5.8_spmd.clone.sunk | while | flops 271778816 | bytes 2167688 | solution.py:125
  14.4 2.7 collective-permute-start
  20.1 2.5 collective-permute-start
  23.2 4.9 %collective-permute-done = bf16[256,2,128]{2,0,1:T(8,128)(2,1)S(1)} collective-permute-done((bf16[256,2,128]{2,0,1:T(8,128)(2,1)S(1)}, bf16[256,2,128]{2,0,1:T(8,128)(2,1)S(1)}, u32[]{:S(2)}, u32[]{:S(2)}) %collective-permute-start) | collective-permute-done | bytes 131104 | tf_op jit(solution)/shard_map/while/body/eval_jaxpr/ppermute | solution.py:15
  29.9 7.1 %collective-permute-done = bf16[256,2,128]{2,0,1:T(8,128)(2,1)S(1)} collective-permute-done((bf16[256,2,128]{2,0,1:T(8,128)(2,1)S(1)}, bf16[256,2,128]{2,0,1:T(8,128)(2,1)S(1)}, u32[]{:S(2)}, u32[]{:S(2)}) %collective-permute-start) | collective-permute-done | bytes 131104 | tf_op jit(solution)/shard_map/while/body/eval_jaxpr/ppermute | solution.py:15
  38.8 7.1 %collective-permute-done = bf16[256,2,128]{2,0,1:T(8,128)(2,1)S(1)} collective-permute-done((bf16[256,2,128]{2,0,1:T(8,128)(2,1)S(1)}, bf16[256,2,128]{2,0,1:T(8,128)(2,1)S(1)}, u32[]{:S(2)}, u32[]{:S(2)}) %collective-permute-start) | collective-permute-done | bytes 131104 | tf_op jit(solution)/shard_map/while/body/eval_jaxpr/ppermute | solution.py:15
  47.6 7.1 %collective-permute-done = bf16[256,2,128]{2,0,1:T(8,128)(2,1)S(1)} collective-permute-done((bf16[256,2,128]{2,0,1:T(8,128)(2,1)S(1)}, bf16[256,2,128]{2,0,1:T(8,128)(2,1)S(1)}, u32[]{:S(2)}, u32[]{:S(2)}) %collective-permute-start) | collective-permute-done | bytes 131104 | tf_op jit(solution)/shard_map/while/body/eval_jaxpr/ppermute | solution.py:15
  56.5 7.1 %collective-permute-done = bf16[256,2,128]{2,0,1:T(8,128)(2,1)S(1)} collective-permute-done((bf16[256,2,128]{2,0,1:T(8,128)(2,1)S(1)}, bf16[256,2,128]{2,0,1:T(8,128)(2,1)S(1)}, u32[]{:S(2)}, u32[]{:S(2)}) %collective-permute-start) | collective-permute-done | bytes 131104 | tf_op jit(solution)/shard_map/while/body/eval_jaxpr/ppermute | solution.py:15
  65.4 7.1 %collective-permute-done = bf16[256,2,128]{2,0,1:T(8,128)(2,1)S(1)} collective-permute-done((bf16[256,2,128]{2,0,1:T(8,128)(2,1)S(1)}, bf16[256,2,128]{2,0,1:T(8,128)(2,1)S(1)}, u32[]{:S(2)}, u32[]{:S(2)}) %collective-permute-start) | collective-permute-done | bytes 131104 | tf_op jit(solution)/shard_map/while/body/eval_jaxpr/ppermute | solution.py:15
  81.3 3.3 fusion.40
  97.4 123.4 %while.39 = (s32[]{:T(128)}, f32[256,2,8,128]{3,0,2,1:T(8,128)S(1)}, f32[256,2,2,128]{3,0,2,1:T(8,128)}, bf16[256,2,2,128]{3,0,2,1:T(8,128)(2,1)}, s32[4,32]{1,0...) while((s32[]{:T(128)}, ...), condition=%wide.region_11.12_spmd.clone, body=%wide.region_9.11_spmd.clone.sunk | while | flops 1354695680 | bytes 37999652 | solution.py:159
  99.1 6.4 %collective-permute-done.1 = bf16[256,2,2,128]{3,0,2,1:T(8,128)(2,1)S(1)} collective-permute-done((bf16[256,2,2,128]{3,0,2,1:T(8,128)(2,1)}, bf16[256,2,2,128]{3,0,2,1:T(8,128)(2,1)S(1)}, u32[]{:S(2)}, u32[]{:S(2)}) %collective-permute-start.1) | collective-permute-done | bytes 262176 | tf_op jit(solution)/shard_map/while/body/eval_jaxpr/ppermute | solution.py:15
  115.7 7.6 %collective-permute-done.1 = bf16[256,2,2,128]{3,0,2,1:T(8,128)(2,1)S(1)} collective-permute-done((bf16[256,2,2,128]{3,0,2,1:T(8,128)(2,1)}, bf16[256,2,2,128]{3,0,2,1:T(8,128)(2,1)S(1)}, u32[]{:S(2)}, u32[]{:S(2)}) %collective-permute-start.1) | collective-permute-done | bytes 262176 | tf_op jit(solution)/shard_map/while/body/eval_jaxpr/ppermute | solution.py:15
  133.5 7.6 %collective-permute-done.1 = bf16[256,2,2,128]{3,0,2,1:T(8,128)(2,1)S(1)} collective-permute-done((bf16[256,2,2,128]{3,0,2,1:T(8,128)(2,1)}, bf16[256,2,2,128]{3,0,2,1:T(8,128)(2,1)S(1)}, u32[]{:S(2)}, u32[]{:S(2)}) %collective-permute-start.1) | collective-permute-done | bytes 262176 | tf_op jit(solution)/shard_map/while/body/eval_jaxpr/ppermute | solution.py:15
  151.3 7.6 %collective-permute-done.1 = bf16[256,2,2,128]{3,0,2,1:T(8,128)(2,1)S(1)} collective-permute-done((bf16[256,2,2,128]{3,0,2,1:T(8,128)(2,1)}, bf16[256,2,2,128]{3,0,2,1:T(8,128)(2,1)S(1)}, u32[]{:S(2)}, u32[]{:S(2)}) %collective-permute-start.1) | collective-permute-done | bytes 262176 | tf_op jit(solution)/shard_map/while/body/eval_jaxpr/ppermute | solution.py:15
  169.1 7.6 %collective-permute-done.1 = bf16[256,2,2,128]{3,0,2,1:T(8,128)(2,1)S(1)} collective-permute-done((bf16[256,2,2,128]{3,0,2,1:T(8,128)(2,1)}, bf16[256,2,2,128]{3,0,2,1:T(8,128)(2,1)S(1)}, u32[]{:S(2)}, u32[]{:S(2)}) %collective-permute-start.1) | collective-permute-done | bytes 262176 | tf_op jit(solution)/shard_map/while/body/eval_jaxpr/ppermute | solution.py:15
  186.9 7.6 %collective-permute-done.1 = bf16[256,2,2,128]{3,0,2,1:T(8,128)(2,1)S(1)} collective-permute-done((bf16[256,2,2,128]{3,0,2,1:T(8,128)(2,1)}, bf16[256,2,2,128]{3,0,2,1:T(8,128)(2,1)S(1)}, u32[]{:S(2)}, u32[]{:S(2)}) %collective-permute-start.1) | collective-permute-done | bytes 262176 | tf_op jit(solution)/shard_map/while/body/eval_jaxpr/ppermute | solution.py:15
  204.7 7.6 %collective-permute-done.1 = bf16[256,2,2,128]{3,0,2,1:T(8,128)(2,1)S(1)} collective-permute-done((bf16[256,2,2,128]{3,0,2,1:T(8,128)(2,1)}, bf16[256,2,2,128]{3,0,2,1:T(8,128)(2,1)S(1)}, u32[]{:S(2)}, u32[]{:S(2)}) %collective-permute-start.1) | collective-permute-done | bytes 262176 | tf_op jit(solution)/shard_map/while/body/eval_jaxpr/ppermute | solution.py:15
  222.3 2.5 multiply_add_fusion
  224.9 2.1 multiply_reduce_fusion.1
  228.3 3.8 %fusion.36 = (f32[2048]{0:T(1024)S(1)}, bf16[256,2048]{1,0:T(8,128)(2,1)}) fusion(bf16[256,2048]{1,0:T(8,128)(2,1)S(1)} %copy-done.3, f32[32,8,16,128]{3,2,1,0:T(8,128)S(1)} %bitcast.265, f32[32,8,16,128]{3,2,1,0:T(8,128)S(1)} %bitcast.267, f32[32,8,16,128]{3,2,1,0:T(8,128)S(1)} %bitcast.266, f32[2048]{0:T(1024)S(1)} %broadcast_bitcast_fusion), kind=kLoop, calls=%fused_computation.53 | loop fusion | flops 4716544 | bytes 8404992 | tf_op jit(solution)/shard_map/reduce_sum | solution.py:59
  235.9 8.7 %all-reduce.1 = (f32[128]{0:T(128)S(1)}, f32[128]{0:T(128)S(1)}) all-reduce(f32[128]{0:T(128)S(1)} %bitcast_reduce_fusion, f32[128]{0:T(128)S(1)} %bitcast_reduce_fusion.1), channel_id=1, replica_groups=mesh['ctx'=64,'heads'=4] {'heads'}, use_global_device_ids=true, to_apply=%region_16.17 | all-reduce | flops 256 | bytes 2048 | tf_op jit(solution)/shard_map/psum | solution.py:166
  244.6 134.0 %all-reduce = (f32[128]{0:T(128)}, f32[128]{0:T(128)}) all-reduce(f32[128]{0:T(128)S(1)} %get-tuple-element.576, f32[128]{0:T(128)S(1)} %get-tuple-element.577), channel_id=1, replica_groups=mesh['ctx'=64,'heads'=4] {'ctx'}, use_global_device_ids=true, to_apply=%region_17.18 | all-reduce | flops 256 | bytes 2048 | tf_op jit(solution)/shard_map/psum | solution.py:166
  (349 shorter events, 121.4 us)
Async XLA Ops:
  1.8 5.1 %copy-start.6 = (f32[256,2,128]{2,0,1:T(8,128)}, f32[256,2,128]{2,0,1:T(8,128)S(1)}, u32[]{:S(2)}) copy-start(f32[256,2,128]{2,0,1:T(8,128)S(1)} %copy.83) | copy-start | bytes 786436
  14.4 59.8 %copy-start.16 = (bf16[256,2048]{1,0:T(8,128)(2,1)S(1)}, bf16[256,2048]{1,0:T(8,128)(2,1)}, u32[]{:S(2)}) copy-start(bf16[256,2048]{1,0:T(8,128)(2,1)} %param.16) | copy-start | bytes 3145732
  14.4 4.6 %collective-permute-start = (bf16[256,2,128]{2,0,1:T(8,128)(2,1)S(1)}, bf16[256,2,128]{2,0,1:T(8,128)(2,1)S(1)}, u32[]{:S(2)}, u32[]{:S(2)}) collective-permute-start(bf16[256,2,128]{2,0,1:T(8,128)(2,1)S(1)} %get-tuple-element.711), channel_id=1, source_target_pairs={{0,4},{4,8},{8,12},{12,16},{16,20},{20,24},{24,28},{28,32},{32,36}... | collective-permute-start | bytes 393224 | tf_op jit(solution)/shard_map/while/body/eval_jaxpr/ppermute | solution.py:15
  20.1 8.0 %collective-permute-start = (bf16[256,2,128]{2,0,1:T(8,128)(2,1)S(1)}, bf16[256,2,128]{2,0,1:T(8,128)(2,1)S(1)}, u32[]{:S(2)}, u32[]{:S(2)}) collective-permute-start(bf16[256,2,128]{2,0,1:T(8,128)(2,1)S(1)} %get-tuple-element.711), channel_id=1, source_target_pairs={{0,4},{4,8},{8,12},{12,16},{16,20},{20,24},{24,28},{28,32},{32,36}... | collective-permute-start | bytes 393224 | tf_op jit(solution)/shard_map/while/body/eval_jaxpr/ppermute | solution.py:15
  29.2 7.8 %collective-permute-start = (bf16[256,2,128]{2,0,1:T(8,128)(2,1)S(1)}, bf16[256,2,128]{2,0,1:T(8,128)(2,1)S(1)}, u32[]{:S(2)}, u32[]{:S(2)}) collective-permute-start(bf16[256,2,128]{2,0,1:T(8,128)(2,1)S(1)} %get-tuple-element.711), channel_id=1, source_target_pairs={{0,4},{4,8},{8,12},{12,16},{16,20},{20,24},{24,28},{28,32},{32,36}... | collective-permute-start | bytes 393224 | tf_op jit(solution)/shard_map/while/body/eval_jaxpr/ppermute | solution.py:15
  38.1 7.8 %collective-permute-start = (bf16[256,2,128]{2,0,1:T(8,128)(2,1)S(1)}, bf16[256,2,128]{2,0,1:T(8,128)(2,1)S(1)}, u32[]{:S(2)}, u32[]{:S(2)}) collective-permute-start(bf16[256,2,128]{2,0,1:T(8,128)(2,1)S(1)} %get-tuple-element.711), channel_id=1, source_target_pairs={{0,4},{4,8},{8,12},{12,16},{16,20},{20,24},{24,28},{28,32},{32,36}... | collective-permute-start | bytes 393224 | tf_op jit(solution)/shard_map/while/body/eval_jaxpr/ppermute | solution.py:15
  47.0 7.8 %collective-permute-start = (bf16[256,2,128]{2,0,1:T(8,128)(2,1)S(1)}, bf16[256,2,128]{2,0,1:T(8,128)(2,1)S(1)}, u32[]{:S(2)}, u32[]{:S(2)}) collective-permute-start(bf16[256,2,128]{2,0,1:T(8,128)(2,1)S(1)} %get-tuple-element.711), channel_id=1, source_target_pairs={{0,4},{4,8},{8,12},{12,16},{16,20},{20,24},{24,28},{28,32},{32,36}... | collective-permute-start | bytes 393224 | tf_op jit(solution)/shard_map/while/body/eval_jaxpr/ppermute | solution.py:15
  55.8 7.8 %collective-permute-start = (bf16[256,2,128]{2,0,1:T(8,128)(2,1)S(1)}, bf16[256,2,128]{2,0,1:T(8,128)(2,1)S(1)}, u32[]{:S(2)}, u32[]{:S(2)}) collective-permute-start(bf16[256,2,128]{2,0,1:T(8,128)(2,1)S(1)} %get-tuple-element.711), channel_id=1, source_target_pairs={{0,4},{4,8},{8,12},{12,16},{16,20},{20,24},{24,28},{28,32},{32,36}... | collective-permute-start | bytes 393224 | tf_op jit(solution)/shard_map/while/body/eval_jaxpr/ppermute | solution.py:15
  64.7 7.8 %collective-permute-start = (bf16[256,2,128]{2,0,1:T(8,128)(2,1)S(1)}, bf16[256,2,128]{2,0,1:T(8,128)(2,1)S(1)}, u32[]{:S(2)}, u32[]{:S(2)}) collective-permute-start(bf16[256,2,128]{2,0,1:T(8,128)(2,1)S(1)} %get-tuple-element.711), channel_id=1, source_target_pairs={{0,4},{4,8},{8,12},{12,16},{16,20},{20,24},{24,28},{28,32},{32,36}... | collective-permute-start | bytes 393224 | tf_op jit(solution)/shard_map/while/body/eval_jaxpr/ppermute | solution.py:15
  97.4 8.1 %collective-permute-start.1 = (bf16[256,2,2,128]{3,0,2,1:T(8,128)(2,1)}, bf16[256,2,2,128]{3,0,2,1:T(8,128)(2,1)S(1)}, u32[]{:S(2)}, u32[]{:S(2)}) collective-permute-start(bf16[256,2,2,128]{3,0,2,1:T(8,128)(2,1)} %get-tuple-element.749), channel_id=1, source_target_pairs={{0,4},{4,8},{8,12},{12,16},{16,20},{20,24},{24,28},{28,32},{32,36}... | collective-permute-start | bytes 786440 | tf_op jit(solution)/shard_map/while/body/eval_jaxpr/ppermute | solution.py:15
  97.4 14.7 %collective-permute-start.2 = (f32[256,2,2,128]{3,0,2,1:T(8,128)}, f32[256,2,2,128]{3,0,2,1:T(8,128)}, u32[]{:S(2)}, u32[]{:S(2)}) collective-permute-start(f32[256,2,2,128]{3,0,2,1:T(8,128)} %get-tuple-element.748), channel_id=1, source_target_pairs={{0,4},{4,8},{8,12},{12,16},{16,20},{20,24},{24,28},{28,32},{32,36}... | collective-permute-start | bytes 1572872 | tf_op jit(solution)/shard_map/while/body/eval_jaxpr/ppermute | solution.py:15
  114.0 9.3 %collective-permute-start.1 = (bf16[256,2,2,128]{3,0,2,1:T(8,128)(2,1)}, bf16[256,2,2,128]{3,0,2,1:T(8,128)(2,1)S(1)}, u32[]{:S(2)}, u32[]{:S(2)}) collective-permute-start(bf16[256,2,2,128]{3,0,2,1:T(8,128)(2,1)} %get-tuple-element.749), channel_id=1, source_target_pairs={{0,4},{4,8},{8,12},{12,16},{16,20},{20,24},{24,28},{28,32},{32,36}... | collective-permute-start | bytes 786440 | tf_op jit(solution)/shard_map/while/body/eval_jaxpr/ppermute | solution.py:15
  114.0 15.9 %collective-permute-start.2 = (f32[256,2,2,128]{3,0,2,1:T(8,128)}, f32[256,2,2,128]{3,0,2,1:T(8,128)}, u32[]{:S(2)}, u32[]{:S(2)}) collective-permute-start(f32[256,2,2,128]{3,0,2,1:T(8,128)} %get-tuple-element.748), channel_id=1, source_target_pairs={{0,4},{4,8},{8,12},{12,16},{16,20},{20,24},{24,28},{28,32},{32,36}... | collective-permute-start | bytes 1572872 | tf_op jit(solution)/shard_map/while/body/eval_jaxpr/ppermute | solution.py:15
  131.8 9.3 %collective-permute-start.1 = (bf16[256,2,2,128]{3,0,2,1:T(8,128)(2,1)}, bf16[256,2,2,128]{3,0,2,1:T(8,128)(2,1)S(1)}, u32[]{:S(2)}, u32[]{:S(2)}) collective-permute-start(bf16[256,2,2,128]{3,0,2,1:T(8,128)(2,1)} %get-tuple-element.749), channel_id=1, source_target_pairs={{0,4},{4,8},{8,12},{12,16},{16,20},{20,24},{24,28},{28,32},{32,36}... | collective-permute-start | bytes 786440 | tf_op jit(solution)/shard_map/while/body/eval_jaxpr/ppermute | solution.py:15
  131.8 15.9 %collective-permute-start.2 = (f32[256,2,2,128]{3,0,2,1:T(8,128)}, f32[256,2,2,128]{3,0,2,1:T(8,128)}, u32[]{:S(2)}, u32[]{:S(2)}) collective-permute-start(f32[256,2,2,128]{3,0,2,1:T(8,128)} %get-tuple-element.748), channel_id=1, source_target_pairs={{0,4},{4,8},{8,12},{12,16},{16,20},{20,24},{24,28},{28,32},{32,36}... | collective-permute-start | bytes 1572872 | tf_op jit(solution)/shard_map/while/body/eval_jaxpr/ppermute | solution.py:15
  149.6 9.3 %collective-permute-start.1 = (bf16[256,2,2,128]{3,0,2,1:T(8,128)(2,1)}, bf16[256,2,2,128]{3,0,2,1:T(8,128)(2,1)S(1)}, u32[]{:S(2)}, u32[]{:S(2)}) collective-permute-start(bf16[256,2,2,128]{3,0,2,1:T(8,128)(2,1)} %get-tuple-element.749), channel_id=1, source_target_pairs={{0,4},{4,8},{8,12},{12,16},{16,20},{20,24},{24,28},{28,32},{32,36}... | collective-permute-start | bytes 786440 | tf_op jit(solution)/shard_map/while/body/eval_jaxpr/ppermute | solution.py:15
  149.6 15.9 %collective-permute-start.2 = (f32[256,2,2,128]{3,0,2,1:T(8,128)}, f32[256,2,2,128]{3,0,2,1:T(8,128)}, u32[]{:S(2)}, u32[]{:S(2)}) collective-permute-start(f32[256,2,2,128]{3,0,2,1:T(8,128)} %get-tuple-element.748), channel_id=1, source_target_pairs={{0,4},{4,8},{8,12},{12,16},{16,20},{20,24},{24,28},{28,32},{32,36}... | collective-permute-start | bytes 1572872 | tf_op jit(solution)/shard_map/while/body/eval_jaxpr/ppermute | solution.py:15
  167.4 9.3 %collective-permute-start.1 = (bf16[256,2,2,128]{3,0,2,1:T(8,128)(2,1)}, bf16[256,2,2,128]{3,0,2,1:T(8,128)(2,1)S(1)}, u32[]{:S(2)}, u32[]{:S(2)}) collective-permute-start(bf16[256,2,2,128]{3,0,2,1:T(8,128)(2,1)} %get-tuple-element.749), channel_id=1, source_target_pairs={{0,4},{4,8},{8,12},{12,16},{16,20},{20,24},{24,28},{28,32},{32,36}... | collective-permute-start | bytes 786440 | tf_op jit(solution)/shard_map/while/body/eval_jaxpr/ppermute | solution.py:15
  167.4 15.9 %collective-permute-start.2 = (f32[256,2,2,128]{3,0,2,1:T(8,128)}, f32[256,2,2,128]{3,0,2,1:T(8,128)}, u32[]{:S(2)}, u32[]{:S(2)}) collective-permute-start(f32[256,2,2,128]{3,0,2,1:T(8,128)} %get-tuple-element.748), channel_id=1, source_target_pairs={{0,4},{4,8},{8,12},{12,16},{16,20},{20,24},{24,28},{28,32},{32,36}... | collective-permute-start | bytes 1572872 | tf_op jit(solution)/shard_map/while/body/eval_jaxpr/ppermute | solution.py:15
  185.2 9.3 %collective-permute-start.1 = (bf16[256,2,2,128]{3,0,2,1:T(8,128)(2,1)}, bf16[256,2,2,128]{3,0,2,1:T(8,128)(2,1)S(1)}, u32[]{:S(2)}, u32[]{:S(2)}) collective-permute-start(bf16[256,2,2,128]{3,0,2,1:T(8,128)(2,1)} %get-tuple-element.749), channel_id=1, source_target_pairs={{0,4},{4,8},{8,12},{12,16},{16,20},{20,24},{24,28},{28,32},{32,36}... | collective-permute-start | bytes 786440 | tf_op jit(solution)/shard_map/while/body/eval_jaxpr/ppermute | solution.py:15
  185.2 15.9 %collective-permute-start.2 = (f32[256,2,2,128]{3,0,2,1:T(8,128)}, f32[256,2,2,128]{3,0,2,1:T(8,128)}, u32[]{:S(2)}, u32[]{:S(2)}) collective-permute-start(f32[256,2,2,128]{3,0,2,1:T(8,128)} %get-tuple-element.748), channel_id=1, source_target_pairs={{0,4},{4,8},{8,12},{12,16},{16,20},{20,24},{24,28},{28,32},{32,36}... | collective-permute-start | bytes 1572872 | tf_op jit(solution)/shard_map/while/body/eval_jaxpr/ppermute | solution.py:15
  203.0 9.3 %collective-permute-start.1 = (bf16[256,2,2,128]{3,0,2,1:T(8,128)(2,1)}, bf16[256,2,2,128]{3,0,2,1:T(8,128)(2,1)S(1)}, u32[]{:S(2)}, u32[]{:S(2)}) collective-permute-start(bf16[256,2,2,128]{3,0,2,1:T(8,128)(2,1)} %get-tuple-element.749), channel_id=1, source_target_pairs={{0,4},{4,8},{8,12},{12,16},{16,20},{20,24},{24,28},{28,32},{32,36}... | collective-permute-start | bytes 786440 | tf_op jit(solution)/shard_map/while/body/eval_jaxpr/ppermute | solution.py:15
  203.0 15.9 %collective-permute-start.2 = (f32[256,2,2,128]{3,0,2,1:T(8,128)}, f32[256,2,2,128]{3,0,2,1:T(8,128)}, u32[]{:S(2)}, u32[]{:S(2)}) collective-permute-start(f32[256,2,2,128]{3,0,2,1:T(8,128)} %get-tuple-element.748), channel_id=1, source_target_pairs={{0,4},{4,8},{8,12},{12,16},{16,20},{20,24},{24,28},{28,32},{32,36}... | collective-permute-start | bytes 1572872 | tf_op jit(solution)/shard_map/while/body/eval_jaxpr/ppermute | solution.py:15
  220.8 11.4 %collective-permute-start.3 = (f32[256,2,2,128]{3,0,2,1:T(8,128)}, f32[256,2,2,128]{3,0,2,1:T(8,128)S(1)}, u32[]{:S(2)}, u32[]{:S(2)}) collective-permute-start(f32[256,2,2,128]{3,0,2,1:T(8,128)} %get-tuple-element.450), channel_id=1, source_target_pairs={{0,228},{4,232},{8,236},{12,240},{16,244},{20,248},{24,252},{28,0}... | collective-permute-start | bytes 1572872 | tf_op jit(solution)/shard_map/ppermute | solution.py:15
  (49 other events, 87.1 us)
